TPU v7x, 512 devices: a whole 4x8x8 slice. The times are simulated.
512 devices in a mesh: dp: 64 (over y, x, core), tensor: 8 (over z).
Axes of the slice: x: 4, y: 8, z: 8, core: 2. Of those that a mesh axis runs over, the one named last changes fastest.
Arguments:
- hidden_act: bfloat16 [32768, 1408], P('dp', 'tensor'), may hold values from -6 to 6
- cotangent: bfloat16 [32768, 2048], P('dp', 'tensor'), may hold values from -4 to 4
- down_table: bfloat16 [1408, 64, 2048], P('tensor', 'dp'), may hold values from -0.15625 to 0.15625
- expert_ids: int32 [128, 4], P('dp'), may hold values from 0 to 31, as said below
- merge_weights: float32 [128, 4], P('dp'), may hold values from 0.1 to 1
- owner_slot: int32 [32], replicated, may hold values from 0 to 63, as said below
Outputs:
- layer_out: bfloat16 [32768, 2048], P('dp', 'tensor')
- grad_hidden: bfloat16 [32768, 1408], P('dp', 'tensor')
- expert_grad: float32 [1408, 64, 2048], P('tensor', 'dp')
Inputs may be any that keep to these rules, and one draw needn't show every extreme that they name: `expert_ids`: each segment lists 4 different experts; the 2 segments of one index of dp list exactly 6 different experts together. `owner_slot`: different experts have different slots; slot 63 always holds an expert.
All inputs are finite; a program needn't handle non-finite values.
Results may differ from a plain program's by a relative error of at most 0.013.
Values may be sent and summed in bfloat16 or wider, within the bound.
A program may use at most 128 MiB of HBM per device.

v0:
```python
import functools
import jax
import jax.numpy as jnp
from jax import lax
from jax.experimental import pallas as pl
from jax.experimental.pallas import tpu as pltpu
from jax.sharding import PartitionSpec as P

K = 4
ROW_PARTS = 4
TILE_ROWS = 16


def two_pieces(values):
    high = lax.reduce_precision(values, 8, 7)
    low = lax.reduce_precision(values - high, 8, 7)
    return high, low


def split_panels(panels, count):
    lead, ff_local, width = panels.shape
    cols = count // ROW_PARTS
    rows = ff_local // ROW_PARTS
    view = panels.reshape(lead, ROW_PARTS, rows, cols, width // cols)
    return jnp.transpose(view, (1, 3, 0, 2, 4)).reshape(count, lead * rows, width // cols)


def join_panels(chunks, lead, rows):
    count, _, lanes = chunks.shape
    cols = count // ROW_PARTS
    view = chunks[:, : lead * rows].reshape(ROW_PARTS, cols, lead, rows, lanes)
    return jnp.transpose(view, (2, 0, 3, 1, 4)).reshape(lead, ROW_PARTS * rows, cols * lanes)


def coefficients(inner, meta_row, listed, seg_count, place_ref):
    count, padded, lanes = inner.shape
    base = (meta_row // TILE_ROWS) * TILE_ROWS
    tail = inner[:, pl.ds(base, TILE_ROWS), :].astype(jnp.float32)
    which = lax.broadcasted_iota(jnp.int32, tail.shape, 1)
    meta = jnp.sum(jnp.where(which == meta_row - base, tail, 0.0), axis=1)
    lane = lax.broadcasted_iota(jnp.int32, (count, lanes), 1).astype(jnp.float32)
    found = []
    for seg in range(seg_count):
        pieces = []
        for piece in (1, 2):
            total = jnp.zeros((count, lanes), jnp.float32)
            for k in range(K):
                at = seg * K + k
                weight = meta[:, piece * listed + at : piece * listed + at + 1]
                total = total + jnp.where(lane == meta[:, at : at + 1], weight, 0.0)
            pieces.append(total)
        rows = jnp.concatenate(pieces, axis=1).astype(jnp.bfloat16)
        found.append(jnp.dot(rows, place_ref[...], preferred_element_type=jnp.float32))
    return jnp.concatenate(found, axis=0).astype(jnp.bfloat16)


def swap_body(sizes, decode, x_ref, aux_ref, wide_ref, *refs):
    rows, lead_in, lead_out = sizes
    gathers = decode is not None
    if gathers:
        out_ref, full_ref, coef_ref, inner, inner_wide, outer_wide, outer = refs[:7]
    else:
        out_ref, sum_ref, inner, inner_wide, outer_wide, outer, held = refs[:7]
    send_one, recv_one, send_two, recv_two, send_side, recv_side = refs[-6:]
    me, side = lax.axis_index("dp"), lax.axis_index("tensor")
    count, padded_in, lanes = x_ref.shape
    padded_out = out_ref.shape[1]
    sides = lax.axis_size("tensor")
    barrier = pltpu.get_barrier_semaphore()

    def greet(step, carry):
        pl.semaphore_signal(
            barrier,
            inc=1,
            device_id={"dp": lax.rem(me + step, count)},
            device_id_type=pl.DeviceIdType.MESH,
        )
        return carry

    def greet_side(step, carry):
        pl.semaphore_signal(
            barrier,
            inc=1,
            device_id={"tensor": lax.rem(side + step, sides)},
            device_id_type=pl.DeviceIdType.MESH,
        )
        return carry

    lax.fori_loop(1, count, greet, 0)
    lax.fori_loop(1, sides, greet_side, 0)
    pl.semaphore_wait(barrier, count + sides - 2)

    def copies(source, target, send_sem, recv_sem):
        def copy(step):
            peer = lax.rem(me + step, count)
            return pltpu.make_async_remote_copy(
                src_ref=source.at[peer],
                dst_ref=target.at[me],
                send_sem=send_sem.at[step],
                recv_sem=recv_sem.at[step],
                device_id={"dp": peer},
                device_id_type=pl.DeviceIdType.MESH,
            )

        return copy

    def stripe(index):
        part = wide_ref.shape[1] if gathers else sum_ref.shape[1]
        return pl.ds(pl.multiple_of(index * part, 128), part)

    def side_copy(step):
        peer = lax.rem(side + step, sides)
        return pltpu.make_async_remote_copy(
            src_ref=wide_ref if gathers else wide_ref.at[:, stripe(peer)],
            dst_ref=full_ref.at[:, stripe(side)] if gathers else held.at[side],
            send_sem=send_side.at[step],
            recv_sem=recv_side.at[step],
            device_id={"tensor": peer},
            device_id_type=pl.DeviceIdType.MESH,
        )

    def begin(copy, steps):
        def one(step, carry):
            copy(step).start()
            return carry

        lax.fori_loop(1, steps, one, 0)

    def finish(copy, steps):
        def one(step, carry):
            copy(step).wait()
            return carry

        lax.fori_loop(1, steps, one, 0)

    first = copies(x_ref, inner, send_one, recv_one)
    begin(first, count)
    begin(side_copy, sides)
    inner[pl.ds(me, 1)] = x_ref[pl.ds(me, 1)]
    if gathers:
        full_ref[:, stripe(side)] = wide_ref[...]
    else:
        held[pl.ds(side, 1)] = wide_ref[:, stripe(side)][None]
    finish(first, count)
    if gathers:
        coef = coefficients(inner, *decode, aux_ref)
        coef_ref[...] = coef
    else:
        coef = aux_ref[...]
    inner_wide[...] = inner[...].astype(jnp.float32).reshape(count * padded_in, lanes)
    outer_wide[...] = jnp.zeros_like(outer_wide)
    for row in range(0, rows, 2):
        pair = jnp.concatenate(
            [
                jnp.concatenate(
                    [
                        inner_wide[pl.ds(seg * rows + row + i, count, stride=padded_in), :]
                        for seg in range(lead_in)
                    ],
                    axis=0,
                )
                for i in (0, 1)
            ],
            axis=1,
        ).astype(jnp.bfloat16)
        summed = jnp.dot(
            coef, jnp.concatenate([pair, pair], axis=0), preferred_element_type=jnp.float32
        )
        for seg in range(lead_out):
            for i in (0, 1):
                outer_wide[pl.ds(seg * rows + row + i, count, stride=padded_out), :] = summed[
                    seg * count : (seg + 1) * count, i * lanes : (i + 1) * lanes
                ]
    outer[...] = outer_wide[...].reshape(count, padded_out, lanes).astype(jnp.bfloat16)
    second = copies(outer, out_ref, send_two, recv_two)
    begin(second, count)
    out_ref[pl.ds(me, 1)] = outer[pl.ds(me, 1)]
    finish(side_copy, sides)
    if not gathers:
        height = 64

        def add_up(block, carry):
            at = pl.ds(pl.multiple_of(block * height, height), height)
            total = held[0, at, :].astype(jnp.float32)
            for other in range(1, sides):
                total = total + held[other, at, :].astype(jnp.float32)
            sum_ref[at, :] = total.astype(sum_ref.dtype)
            return carry

        lax.fori_loop(0, sum_ref.shape[0] // height, add_up, 0)
    finish(second, count)


def swap(blocks, aux, wide, rows, lead_in, lead_out, decode, collective_id):
    count, padded_in, lanes = blocks.shape
    padded_out = -(-lead_out * rows // 8) * 8
    sides = lax.axis_size("tensor")
    tall, across = wide.shape
    if decode is not None:
        side_shapes = (
            jax.ShapeDtypeStruct((tall, across * sides), jnp.bfloat16),
            jax.ShapeDtypeStruct((lead_out * count, 2 * count), jnp.bfloat16),
        )
        holds = []
    else:
        side_shapes = (jax.ShapeDtypeStruct((tall, across // sides), jnp.bfloat16),)
        holds = [pltpu.VMEM((sides, tall, across // sides), jnp.bfloat16)]
    results = (jax.ShapeDtypeStruct((count, padded_out, lanes), jnp.bfloat16),) + side_shapes
    vmem = pl.BlockSpec(memory_space=pltpu.VMEM)
    return pl.pallas_call(
        functools.partial(swap_body, (rows, lead_in, lead_out), decode),
        out_shape=results,
        in_specs=[vmem] * 3,
        out_specs=(vmem,) * len(results),
        scratch_shapes=[
            pltpu.VMEM((count, padded_in, lanes), jnp.bfloat16),
            pltpu.VMEM((count * padded_in, lanes), jnp.float32),
            pltpu.VMEM((count * padded_out, lanes), jnp.float32),
            pltpu.VMEM((count, padded_out, lanes), jnp.bfloat16),
        ]
        + holds
        + [pltpu.SemaphoreType.DMA((count,))] * 4
        + [pltpu.SemaphoreType.DMA((sides,))] * 2,
        compiler_params=pltpu.CompilerParams(
            collective_id=collective_id, has_side_effects=True, vmem_limit_bytes=40 * 1024 * 1024
        ),
    )(blocks, aux, wide)


def body(hidden_act, cotangent, down_table, expert_ids, merge_weights, owner_slot):
    count = lax.axis_size("dp")
    seg_count = expert_ids.shape[0]
    ff_local, _, width = down_table.shape
    row_count = hidden_act.shape[0]
    seg_len = row_count // seg_count
    rows = ff_local // ROW_PARTS
    padded = -(-(rows + 1) // 8) * 8
    lanes = width * ROW_PARTS // count
    listed = seg_count * K

    high, low = two_pieces(merge_weights)
    meta = jnp.concatenate(
        [expert_ids.astype(jnp.float32).reshape(-1), high.reshape(-1), low.reshape(-1)]
    ).astype(jnp.bfloat16)
    meta = jnp.pad(meta[None, :], ((0, padded - rows - 1), (0, lanes - 3 * listed)))
    table_chunks = split_panels(jnp.transpose(down_table, (1, 0, 2)), count)
    outgoing = jnp.concatenate(
        [table_chunks, jnp.broadcast_to(meta, (count,) + meta.shape)], axis=1
    )
    slot_range = jnp.arange(count, dtype=jnp.int32)
    place = jnp.pad(
        (owner_slot[:, None] == slot_range[None, :]).astype(jnp.bfloat16),
        ((0, lanes - owner_slot.shape[0]), (0, 0)),
    )
    nothing = jnp.zeros_like(place)
    place_two = jnp.concatenate(
        [
            jnp.concatenate([place, nothing], axis=1),
            jnp.concatenate([nothing, place], axis=1),
        ],
        axis=0,
    )
    merged_chunks, full_cot, coef = swap(
        outgoing, place_two, cotangent, rows, 1, seg_count, (rows, listed, seg_count), 0
    )
    merged = join_panels(merged_chunks, seg_count, rows)

    hidden_seg = hidden_act.reshape(seg_count, seg_len, ff_local)
    cot_seg = full_cot.reshape(seg_count, seg_len, width)
    seg_grads = jnp.einsum(
        "stf,std->sfd", hidden_seg, cot_seg, preferred_element_type=jnp.float32
    ).astype(jnp.bfloat16)

    partial_rows = jnp.einsum(
        "stf,sfd->std", hidden_seg, merged, preferred_element_type=jnp.float32
    ).reshape(row_count, width)
    grad_hidden = (
        jnp.einsum("std,sfd->stf", cot_seg, merged, preferred_element_type=jnp.float32)
        .astype(jnp.bfloat16)
        .reshape(row_count, ff_local)
    )

    by_segment = jnp.transpose(
        coef.reshape(seg_count * count, 2, count), (2, 1, 0)
    ).reshape(count, 2 * seg_count * count)
    slot_chunks, layer_out = swap(
        split_panels(seg_grads, count),
        by_segment,
        partial_rows.astype(jnp.bfloat16),
        rows,
        seg_count,
        1,
        None,
        1,
    )
    own_grad = join_panels(slot_chunks, 1, rows)
    expert_grad = jnp.transpose(own_grad, (1, 0, 2)).astype(jnp.float32)
    return (layer_out, grad_hidden, expert_grad)


def solution(mesh):
    placed = (
        P("dp", "tensor"),
        P("dp", "tensor"),
        P("tensor", "dp", None),
        P("dp", None),
        P("dp", None),
        P(),
    )
    return jax.shard_map(
        body,
        mesh=mesh,
        in_specs=placed,
        out_specs=(P("dp", "tensor"), P("dp", "tensor"), P("tensor", "dp", None)),
        check_vma=False,
    )
```

profile of v0, /device:TPU:1, one launch (start us, length us, event | category | flops | bytes accessed | tf_op | source)
XLA Modules:
  0.0 164.6 jit_solution(7676527403337319833)
XLA Ops:
  0.6 0.7 convert_convert_fusion
  1.4 0.7 reduce-precision_convert_fusion
  2.3 0.7 iota_compare_fusion.2
  3.2 1.3 copy.40
  4.5 0.2 copy.26
  4.8 0.6 copy-done.2
  5.4 71.0 %shard_map.85 = (bf16[64,88,128]{2,1,0:T(8,128)(2,1)S(1)}, bf16[512,2048]{1,0:T(8,128)(2,1)S(1)}, bf16[128,128]{1,0:T(8,128)(2,1)S(1)}) custom-call(bf16[64,48,128]{2,1,0:T(8,128)(2,1)S(1)} %pad_maximum_fusion.x_ref, bf16[256,128]{1,0:T(8,128)(2,1)S(1)} %fusion.7.aux_ref, bf16[512,256]{1,0:T(8,128)(2,1)S(1)} %copy-done.2), custom_call_target="tpu_custom_call" | custom-call | tf_op jit(solution)/shard_map/pallas_call | solution.py:210
  76.4 1.1 copy-done
  77.6 0.6 copy.51
  78.2 0.5 convolution_convert_fusion.1
  78.8 0.4 copy.41
  79.1 0.4 copy.28
  79.6 0.9 copy.34.x_ref
  80.5 0.4 copy-done.1
  80.9 0.4 copy.31
  81.3 1.4 copy.32
  82.7 3.5 %reshape.115 = bf16[2,176,2048]{2,1,0:T(8,128)(2,1)} reshape(bf16[2,4,44,16,128]{4,3,2,1,0:T(8,128)(2,1)} %copy.32) | data formatting | bytes 2883584 | tf_op jit(solution)/shard_map/reshape | solution.py:32
  86.2 2.3 %fusion = bf16[2,22,8,256]{3,2,1,0:T(8,128)(2,1)S(1)} fusion(bf16[2,256,2048]{2,1,0:T(8,128)(2,1)S(1)} %bitcast.53, bf16[2,176,2048]{2,1,0:T(8,128)(2,1)} %reshape.115), kind=kOutput, calls=%fused_computation.4 | convolution fusion | flops 369188864 | bytes 3719168 | tf_op jit(solution)/shard_map/std,sfd->stf/dot_general | solution.py:278
  88.5 0.7 copy.39
  89.2 0.8 convolution_convert_fusion
  90.0 72.3 %shard_map.86 = (bf16[64,48,128]{2,1,0:T(8,128)(2,1)S(1)}, bf16[512,256]{1,0:T(8,128)(2,1)S(1)}) custom-call(bf16[64,88,128]{2,1,0:T(8,128)(2,1)S(1)} %copy.34.x_ref, bf16[64,256]{1,0:T(8,128)(2,1)S(1)} %bitcast.55, bf16[512,2048]{1,0:T(8,128)(2,1)S(1)} %bitcast.51), custom_call_target="tpu_custom_call" | custom-call | tf_op jit(solution)/shard_map/pallas_call | solution.py:210
  162.2 0.1 convert_bitcast_fusion
  162.4 1.5 copy.36
  163.9 0.7 copy.53
  (20 shorter events, 0.7 us)
Async XLA Ops:
  4.4 1.0 copy-start.2
  4.7 73.6 %copy-start.5 = (bf16[512,176]{0,1:T(8,128)(2,1)S(1)}, bf16[512,176]{0,1:T(8,128)(2,1)}, u32[]{:S(2)}) copy-start(bf16[512,176]{0,1:T(8,128)(2,1)} %param.6) | copy-start | bytes 540676
  76.4 1.1 copy-start
  79.6 1.4 copy-start.1
  86.2 3.0 %copy-start.4 = (bf16[2,176,2048]{2,1,0:T(8,128)(2,1)S(1)}, bf16[2,176,2048]{2,1,0:T(8,128)(2,1)}, u32[]{:S(2)}) copy-start(bf16[2,176,2048]{2,1,0:T(8,128)(2,1)} %reshape.115) | copy-start | bytes 4325380
  86.2 3.0 %copy-start.6 = (bf16[512,176]{0,1:T(8,128)(2,1)S(1)}, bf16[512,176]{0,1:T(8,128)(2,1)}, u32[]{:S(2)}) copy-start(bf16[512,176]{0,1:T(8,128)(2,1)} %param.6) | copy-start | bytes 540676
  89.2 0.8 copy-start.3
where the time goes:
time: 165 us
  Pallas kernels  143 us (87%)
  local copies, waits for them, and re-layouts  14.5 us (9%)
  matrix products  3.63 us (2%)
  other arithmetic  2.52 us (2%)
    pallas_call x2, Pallas kernels, swap(): pl.pallas_call(functools.partial(swap_body, (rows, lead_in, lead_out), de...  143 us
    unnamed x17, local copies, waits for them, and re-layouts  4.45 us
    reshape x1, local copies, waits for them, and re-layouts, join_panels(): jnp.transpose(view, (2, 0, 3, 1, 4))  3.5 us

commit v1 on v0

v1 whole, which is shorter than its diff:
```python
import functools
import jax
import jax.numpy as jnp
from jax import lax
from jax.experimental import pallas as pl
from jax.experimental.pallas import tpu as pltpu
from jax.sharding import PartitionSpec as P

K = 4
ROW_PARTS = 4
TILE_ROWS = 16


def two_pieces(values):
    high = lax.reduce_precision(values, 8, 7)
    low = lax.reduce_precision(values - high, 8, 7)
    return high, low


def split_panels(panels, count):
    lead, ff_local, width = panels.shape
    cols = count // ROW_PARTS
    rows = ff_local // ROW_PARTS
    view = panels.reshape(lead, ROW_PARTS, rows, cols, width // cols)
    return jnp.transpose(view, (1, 3, 0, 2, 4)).reshape(count, lead * rows, width // cols)


def join_panels(chunks, lead, rows):
    count, _, lanes = chunks.shape
    cols = count // ROW_PARTS
    view = chunks[:, : lead * rows].reshape(ROW_PARTS, cols, lead, rows, lanes)
    return jnp.transpose(view, (2, 0, 3, 1, 4)).reshape(lead, ROW_PARTS * rows, cols * lanes)


def coefficients(inner, meta_row, listed, seg_count, place_ref):
    count, padded, lanes = inner.shape
    base = (meta_row // TILE_ROWS) * TILE_ROWS
    tail = inner[:, pl.ds(base, TILE_ROWS), :].astype(jnp.float32)
    which = lax.broadcasted_iota(jnp.int32, tail.shape, 1)
    meta = jnp.sum(jnp.where(which == meta_row - base, tail, 0.0), axis=1)
    lane = lax.broadcasted_iota(jnp.int32, (count, lanes), 1).astype(jnp.float32)
    found = []
    for seg in range(seg_count):
        pieces = []
        for piece in (1, 2):
            total = jnp.zeros((count, lanes), jnp.float32)
            for k in range(K):
                at = seg * K + k
                weight = meta[:, piece * listed + at : piece * listed + at + 1]
                total = total + jnp.where(lane == meta[:, at : at + 1], weight, 0.0)
            pieces.append(total)
        rows = jnp.concatenate(pieces, axis=1).astype(jnp.bfloat16)
        found.append(jnp.dot(rows, place_ref[...], preferred_element_type=jnp.float32))
    return jnp.concatenate(found, axis=0)


def step_body(
    rows, seg_count, decode, x_ref, place_ref, cot_ref, hid_ref, hid_t_ref,
    slot_ref, layer_ref, grad_ref,
    full, in_one, in_two, in_three, held, wide_one, wide_two, out_two, out_three, out_four,
    merged, partial, *sems
):
    me, side = lax.axis_index("dp"), lax.axis_index("tensor")
    count, padded, lanes = x_ref.shape
    tall, part = cot_ref.shape
    width = full.shape[1]
    sides = lax.axis_size("tensor")
    both = seg_count * rows
    cols = count // ROW_PARTS
    pair_lanes = 2 * lanes
    barrier = pltpu.get_barrier_semaphore()

    def greet(step, carry):
        pl.semaphore_signal(
            barrier,
            inc=1,
            device_id={"dp": lax.rem(me + step, count)},
            device_id_type=pl.DeviceIdType.MESH,
        )
        return carry

    def greet_side(step, carry):
        pl.semaphore_signal(
            barrier,
            inc=1,
            device_id={"tensor": lax.rem(side + step, sides)},
            device_id_type=pl.DeviceIdType.MESH,
        )
        return carry

    lax.fori_loop(1, count, greet, 0)
    lax.fori_loop(1, sides, greet_side, 0)
    pl.semaphore_wait(barrier, count + sides - 2)

    def copies(source, target, send_sem, recv_sem):
        def copy(step):
            peer = lax.rem(me + step, count)
            return pltpu.make_async_remote_copy(
                src_ref=source.at[peer],
                dst_ref=target.at[me],
                send_sem=send_sem.at[step],
                recv_sem=recv_sem.at[step],
                device_id={"dp": peer},
                device_id_type=pl.DeviceIdType.MESH,
            )

        return copy

    def stripe(index):
        return pl.ds(pl.multiple_of(index * part, 128), part)

    def gather_copy(step):
        return pltpu.make_async_remote_copy(
            src_ref=cot_ref,
            dst_ref=full.at[:, stripe(side)],
            send_sem=sems[8].at[step],
            recv_sem=sems[9].at[step],
            device_id={"tensor": lax.rem(side + step, sides)},
            device_id_type=pl.DeviceIdType.MESH,
        )

    def scatter_copy(step):
        peer = lax.rem(side + step, sides)
        return pltpu.make_async_remote_copy(
            src_ref=partial.at[:, stripe(peer)],
            dst_ref=held.at[side],
            send_sem=sems[10].at[step],
            recv_sem=sems[11].at[step],
            device_id={"tensor": peer},
            device_id_type=pl.DeviceIdType.MESH,
        )

    def begin(copy, steps):
        def one(step, carry):
            copy(step).start()
            return carry

        lax.fori_loop(1, steps, one, 0)

    def finish(copy, steps):
        def one(step, carry):
            copy(step).wait()
            return carry

        lax.fori_loop(1, steps, one, 0)

    def mix(coef, source, target, lead_in, lead_out, high_in, high_out):
        for row in range(0, rows, 2):
            pair = jnp.concatenate(
                [
                    jnp.concatenate(
                        [
                            source[pl.ds(seg * rows + row + i, count, stride=high_in), :]
                            for seg in range(lead_in)
                        ],
                        axis=0,
                    )
                    for i in (0, 1)
                ],
                axis=1,
            ).astype(jnp.bfloat16)
            summed = jnp.dot(
                coef, jnp.concatenate([pair, pair], axis=0), preferred_element_type=jnp.float32
            )
            for seg in range(lead_out):
                for i in (0, 1):
                    target[pl.ds(seg * rows + row + i, count, stride=high_out), :] = summed[
                        seg * count : (seg + 1) * count, i * lanes : (i + 1) * lanes
                    ]

    first = copies(x_ref, in_one, sems[0], sems[1])
    second = copies(out_two, in_two, sems[2], sems[3])
    third = copies(out_three, in_three, sems[4], sems[5])
    fourth = copies(out_four, slot_ref, sems[6], sems[7])

    begin(first, count)
    begin(gather_copy, sides)
    in_one[pl.ds(me, 1)] = x_ref[pl.ds(me, 1)]
    full[:, stripe(side)] = cot_ref[...]
    finish(first, count)

    coef = coefficients(in_one, *decode, place_ref)
    wide_one[...] = in_one[...].astype(jnp.float32).reshape(count * padded, lanes)
    mix(coef.astype(jnp.bfloat16), wide_one, wide_two, 1, seg_count, padded, both)
    out_two[...] = wide_two[...].reshape(count, both, lanes).astype(jnp.bfloat16)
    begin(second, count)
    in_two[pl.ds(me, 1)] = out_two[pl.ds(me, 1)]

    finish(gather_copy, sides)

    def seg_grads(block, carry):
        at = pl.ds(pl.multiple_of(block * pair_lanes, pair_lanes), pair_lanes)
        product = jnp.dot(hid_t_ref[...], full[:, at], preferred_element_type=jnp.float32)
        for up in range(ROW_PARTS):
            for i in (0, 1):
                out_three[pl.ds(up * cols + block * 2 + i, 1)] = product[
                    up * both : (up + 1) * both, i * lanes : (i + 1) * lanes
                ].astype(jnp.bfloat16)[None]
        return carry

    lax.fori_loop(0, width // pair_lanes, seg_grads, 0)
    begin(third, count)
    in_three[pl.ds(me, 1)] = out_three[pl.ds(me, 1)]

    finish(second, count)
    wide_two[...] = in_two[...].astype(jnp.float32).reshape(count * both, lanes)

    def forward(block, carry):
        at = pl.ds(pl.multiple_of(block * pair_lanes, pair_lanes), pair_lanes)
        panel = jnp.concatenate(
            [
                jnp.concatenate(
                    [
                        wide_two[
                            pl.ds(
                                pl.multiple_of((up * cols + block * 2 + i) * both, 8), both
                            ),
                            :,
                        ]
                        for up in range(ROW_PARTS)
                    ],
                    axis=0,
                )
                for i in (0, 1)
            ],
            axis=1,
        ).astype(jnp.bfloat16)
        merged[:, at] = panel
        partial[:, at] = jnp.dot(
            hid_ref[...], panel, preferred_element_type=jnp.float32
        ).astype(jnp.bfloat16)
        return carry

    lax.fori_loop(0, width // pair_lanes, forward, 0)
    begin(scatter_copy, sides)
    held[pl.ds(side, 1)] = partial[:, stripe(side)][None]

    height = 64

    def backward(block, carry):
        at = pl.ds(pl.multiple_of(block * height, height), height)
        grad_ref[at, :] = lax.dot_general(
            full[at, :],
            merged[...],
            (((1,), (1,)), ((), ())),
            preferred_element_type=jnp.float32,
        ).astype(jnp.bfloat16)
        return carry

    lax.fori_loop(0, tall // height, backward, 0)

    finish(third, count)
    turned = jnp.transpose(coef)
    by_segment = jnp.concatenate([turned[:count], turned[count:]], axis=1)
    wide_two[...] = in_three[...].astype(jnp.float32).reshape(count * both, lanes)
    wide_one[...] = jnp.zeros_like(wide_one)
    mix(by_segment.astype(jnp.bfloat16), wide_two, wide_one, seg_count, 1, both, padded)
    out_four[...] = wide_one[...].reshape(count, padded, lanes).astype(jnp.bfloat16)
    begin(fourth, count)
    slot_ref[pl.ds(me, 1)] = out_four[pl.ds(me, 1)]

    finish(scatter_copy, sides)

    def add_up(block, carry):
        at = pl.ds(pl.multiple_of(block * height, height), height)
        total = held[0, at, :].astype(jnp.float32)
        for other in range(1, sides):
            total = total + held[other, at, :].astype(jnp.float32)
        layer_ref[at, :] = total.astype(jnp.bfloat16)
        return carry

    lax.fori_loop(0, tall // height, add_up, 0)
    finish(fourth, count)


def whole_step(blocks, place, cotangent, hidden, hidden_t, rows, seg_count, decode):
    count, padded, lanes = blocks.shape
    sides = lax.axis_size("tensor")
    tall, part = cotangent.shape
    both = seg_count * rows
    high = ROW_PARTS * both
    vmem = pl.BlockSpec(memory_space=pltpu.VMEM)
    narrow = functools.partial(pltpu.VMEM, dtype=jnp.bfloat16)
    results = tuple(
        jax.ShapeDtypeStruct(shape, jnp.bfloat16)
        for shape in ((count, padded, lanes), (tall, part), (tall, high))
    )
    return pl.pallas_call(
        functools.partial(step_body, rows, seg_count, decode),
        out_shape=results,
        in_specs=[vmem] * 5,
        out_specs=(vmem,) * 3,
        scratch_shapes=[
            narrow((tall, part * sides)),
            narrow((count, padded, lanes)),
            narrow((count, both, lanes)),
            narrow((count, both, lanes)),
            narrow((sides, tall, part)),
            pltpu.VMEM((count * padded, lanes), jnp.float32),
            pltpu.VMEM((count * both, lanes), jnp.float32),
            narrow((count, both, lanes)),
            narrow((count, both, lanes)),
            narrow((count, padded, lanes)),
            narrow((high, part * sides)),
            narrow((tall, part * sides)),
        ]
        + [pltpu.SemaphoreType.DMA((count,))] * 8
        + [pltpu.SemaphoreType.DMA((sides,))] * 4,
        compiler_params=pltpu.CompilerParams(
            collective_id=0, has_side_effects=True, vmem_limit_bytes=56 * 1024 * 1024
        ),
    )(blocks, place, cotangent, hidden, hidden_t)


def body(hidden_act, cotangent, down_table, expert_ids, merge_weights, owner_slot):
    count = lax.axis_size("dp")
    seg_count = expert_ids.shape[0]
    ff_local, _, width = down_table.shape
    row_count = hidden_act.shape[0]
    seg_len = row_count // seg_count
    rows = ff_local // ROW_PARTS
    padded = -(-(rows + 1) // 8) * 8
    lanes = width * ROW_PARTS // count
    listed = seg_count * K

    high, low = two_pieces(merge_weights)
    meta = jnp.concatenate(
        [expert_ids.astype(jnp.float32).reshape(-1), high.reshape(-1), low.reshape(-1)]
    ).astype(jnp.bfloat16)
    meta = jnp.pad(meta[None, :], ((0, padded - rows - 1), (0, lanes - 3 * listed)))
    table_chunks = split_panels(jnp.transpose(down_table, (1, 0, 2)), count)
    outgoing = jnp.concatenate(
        [table_chunks, jnp.broadcast_to(meta, (count,) + meta.shape)], axis=1
    )
    slot_range = jnp.arange(count, dtype=jnp.int32)
    place = jnp.pad(
        (owner_slot[:, None] == slot_range[None, :]).astype(jnp.bfloat16),
        ((0, lanes - owner_slot.shape[0]), (0, 0)),
    )
    nothing = jnp.zeros_like(place)
    place_two = jnp.concatenate(
        [
            jnp.concatenate([place, nothing], axis=1),
            jnp.concatenate([nothing, place], axis=1),
        ],
        axis=0,
    )
    parts = hidden_act.reshape(seg_count, seg_len, ROW_PARTS, 1, rows)
    same = jnp.eye(seg_count, dtype=jnp.bool_)[:, None, None, :, None]
    hidden = jnp.where(same, parts, 0).reshape(row_count, ROW_PARTS * seg_count * rows)
    slot_chunks, layer_out, grad_all = whole_step(
        outgoing,
        place_two,
        cotangent,
        hidden,
        hidden.T,
        rows,
        seg_count,
        (rows, listed, seg_count),
    )
    grad_view = grad_all.reshape(seg_count, seg_len, ROW_PARTS, seg_count, rows)
    grad_hidden = jnp.stack(
        [grad_view[seg, :, :, seg] for seg in range(seg_count)]
    ).reshape(row_count, ff_local)
    own_grad = join_panels(slot_chunks, 1, rows)
    expert_grad = jnp.transpose(own_grad, (1, 0, 2)).astype(jnp.float32)
    return (layer_out, grad_hidden, expert_grad)


def solution(mesh):
    placed = (
        P("dp", "tensor"),
        P("dp", "tensor"),
        P("tensor", "dp", None),
        P("dp", None),
        P("dp", None),
        P(),
    )
    return jax.shard_map(
        body,
        mesh=mesh,
        in_specs=placed,
        out_specs=(P("dp", "tensor"), P("dp", "tensor"), P("tensor", "dp", None)),
        check_vma=False,
    )
```

time: 165 us -> 148 us (0.90)
  the two profiles are of different devices: /device:TPU:1 before, /device:TPU:143 now
where the time goes in v1:
time: 148 us
  Pallas kernels  135 us (91%)
  local copies, waits for them, and re-layouts  7.32 us (5%)
  other arithmetic  4.56 us (3%)
    pallas_call x1, Pallas kernels, whole_step(): pl.pallas_call(functools.partial(step_body, rows, seg_count, decode), out...  135 us

profile of v1, /device:TPU:143, one launch (start us, length us, event | category | flops | bytes accessed | tf_op | source)
XLA Modules:
  0.0 148.0 jit_solution(8660317981448174293)
XLA Ops:
  0.6 0.8 convert_convert_fusion
  1.4 0.1 concatenate.29
  1.5 0.7 reduce-precision_convert_fusion
  2.2 0.1 concatenate.30
  2.3 0.1 concatenate.31
  2.4 0.7 iota_compare_fusion.2
  3.2 0.7 fusion.2.place_ref
  3.9 1.0 broadcast_in_dim.32
  4.9 0.3 broadcast_select_fusion
  5.3 0.9 copy.21.hid_ref
  6.2 0.1 copy.27
  6.4 0.2 copy.20
  6.6 1.0 pad_maximum_fusion.x_ref
  7.6 135.4 %shard_map.85 = (bf16[64,48,128]{2,1,0:T(8,128)(2,1)}, bf16[512,256]{1,0:T(8,128)(2,1)}, bf16[512,352]{1,0:T(8,128)(2,1)}) custom-call(bf16[64,48,128]{2,1,0:T(8,128)(2,1)} %pad_maximum_fusion.x_ref, bf16[256,128]{1,0:T(8,128)(2,1)} %fusion.2.place_ref, bf16[512,256]{1,0:T(8,128)(2,1)} %cot_ref.1, bf16[512,352]{1,0:T(8,128)(2,1)} %copy.21.hid_ref, ...), custom_call_target="tpu_custom_call" | custom-call | tf_op jit(solution)/shard_map/pallas_call | solution.py:288
  142.9 1.2 copy.22
  144.1 0.1 reshape.99
  144.2 0.3 fusion.14
  144.5 0.1 copy_bitcast_fusion
  144.6 0.1 pad_maximum_fusion.1
  144.8 0.1 copy.25
  144.9 0.7 copy.29
  145.6 0.1 convert_bitcast_fusion
  145.8 1.5 %copy.26 = f32[1,4,44,16,128]{4,3,2,1,0:T(8,128)} copy(f32[1,4,44,16,128]{4,2,3,1,0:T(8,128)S(1)} %convert_bitcast_fusion) | data formatting | bytes 2883584 | tf_op jit(solution)/shard_map/convert_element_type | solution.py:366
  147.3 0.7 copy.33
  (13 shorter events, 0.2 us)
Async XLA Ops:
  0.6 5.6 %copy-start.2 = (bf16[176,1,2048]{2,0,1:T(8,128)(2,1)S(1)}, bf16[176,1,2048]{2,0,1:T(8,128)(2,1)}, u32[]{:S(2)}) copy-start(bf16[176,1,2048]{2,0,1:T(8,128)(2,1)} %param.8) | copy-start | bytes 2162692
  5.3 1.3 copy-start
  144.1 1.5 %copy-start.1 = (bf16[64,48,128]{2,1,0:T(8,128)(2,1)S(1)}, bf16[64,48,128]{2,1,0:T(8,128)(2,1)}, u32[]{:S(2)}) copy-start(bf16[64,48,128]{2,1,0:T(8,128)(2,1)} %get-tuple-element.8) | copy-start | bytes 2359300
  145.7 1.6 %copy-start.3 = (bf16[512,256]{1,0:T(8,128)(2,1)S(1)}, bf16[512,256]{1,0:T(8,128)(2,1)}, u32[]{:S(2)}) copy-start(bf16[512,256]{1,0:T(8,128)(2,1)} %get-tuple-element.18) | copy-start | bytes 786436

commit v2 on v1

--- a/solution.py
+++ b/solution.py
@@ -26,9 +26,9 @@
 
 
 def join_panels(chunks, lead, rows):
-    count, _, lanes = chunks.shape
+    count, high, lanes = chunks.shape
     cols = count // ROW_PARTS
-    view = chunks[:, : lead * rows].reshape(ROW_PARTS, cols, lead, rows, lanes)
+    view = chunks[:, high - lead * rows :].reshape(ROW_PARTS, cols, lead, rows, lanes)
     return jnp.transpose(view, (2, 0, 3, 1, 4)).reshape(lead, ROW_PARTS * rows, cols * lanes)
 
 
@@ -92,14 +92,20 @@
     lax.fori_loop(1, sides, greet_side, 0)
     pl.semaphore_wait(barrier, count + sides - 2)
 
-    def copies(source, target, send_sem, recv_sem):
+    half = padded // 2
+    cut = half - (padded - rows)
+    slim = ((0, half), (half, half))
+    double = ((0, seg_count * cut), (seg_count * cut, seg_count * (rows - cut)))
+
+    def copies(source, target, send_sem, recv_sem, piece, piece_index):
         def copy(step):
             peer = lax.rem(me + step, count)
+            mark = piece_index * count + step
             return pltpu.make_async_remote_copy(
-                src_ref=source.at[peer],
-                dst_ref=target.at[me],
-                send_sem=send_sem.at[step],
-                recv_sem=recv_sem.at[step],
+                src_ref=source.at[peer, pl.ds(*piece)],
+                dst_ref=target.at[me, pl.ds(*piece)],
+                send_sem=send_sem.at[mark],
+                recv_sem=recv_sem.at[mark],
                 device_id={"dp": peer},
                 device_id_type=pl.DeviceIdType.MESH,
             )
@@ -144,13 +150,27 @@
 
         lax.fori_loop(1, steps, one, 0)
 
-    def mix(coef, source, target, lead_in, lead_out, high_in, high_out):
-        for row in range(0, rows, 2):
+    def spot(piece, seg, row, lead):
+        if lead == 1:
+            return row + padded - rows - piece * half
+        return seg * (rows - cut) + row - cut if piece else seg * cut + row
+
+    def mix(coef, piece, source, target, lead_in, lead_out):
+        start_in, high_in = (double if lead_in > 1 else slim)[piece]
+        start_out, high_out = (double if lead_out > 1 else slim)[piece]
+        for row in range(cut if piece else 0, rows if piece else cut, 2):
             pair = jnp.concatenate(
                 [
                     jnp.concatenate(
                         [
-                            source[pl.ds(seg * rows + row + i, count, stride=high_in), :]
+                            source[
+                                pl.ds(
+                                    count * start_in + spot(piece, seg, row + i, lead_in),
+                                    count,
+                                    stride=high_in,
+                                ),
+                                :,
+                            ]
                             for seg in range(lead_in)
                         ],
                         axis=0,
@@ -164,26 +184,48 @@
             )
             for seg in range(lead_out):
                 for i in (0, 1):
-                    target[pl.ds(seg * rows + row + i, count, stride=high_out), :] = summed[
-                        seg * count : (seg + 1) * count, i * lanes : (i + 1) * lanes
-                    ]
-
-    first = copies(x_ref, in_one, sems[0], sems[1])
-    second = copies(out_two, in_two, sems[2], sems[3])
-    third = copies(out_three, in_three, sems[4], sems[5])
-    fourth = copies(out_four, slot_ref, sems[6], sems[7])
-
-    begin(first, count)
+                    target[
+                        pl.ds(
+                            count * start_out + spot(piece, seg, row + i, lead_out),
+                            count,
+                            stride=high_out,
+                        ),
+                        :,
+                    ] = summed[seg * count : (seg + 1) * count, i * lanes : (i + 1) * lanes]
+
+    def widen(source, target, piece):
+        start, high = piece
+        target[pl.ds(count * start, count * high), :] = (
+            source[:, pl.ds(start, high), :].astype(jnp.float32).reshape(count * high, lanes)
+        )
+
+    def narrow(source, target, piece):
+        start, high = piece
+        target[:, pl.ds(start, high), :] = (
+            source[pl.ds(count * start, count * high), :]
+            .reshape(count, high, lanes)
+            .astype(jnp.bfloat16)
+        )
+
+    first = [copies(x_ref, in_one, sems[0], sems[1], slim[p], p) for p in (0, 1)]
+    second = [copies(out_two, in_two, sems[2], sems[3], double[p], p) for p in (0, 1)]
+    third = [copies(out_three, in_three, sems[4], sems[5], double[p], p) for p in (0, 1)]
+    fourth = [copies(out_four, slot_ref, sems[6], sems[7], slim[p], p) for p in (0, 1)]
+
+    begin(first[0], count)
+    begin(first[1], count)
     begin(gather_copy, sides)
     in_one[pl.ds(me, 1)] = x_ref[pl.ds(me, 1)]
     full[:, stripe(side)] = cot_ref[...]
-    finish(first, count)
-
+    finish(first[0], count)
     coef = coefficients(in_one, *decode, place_ref)
-    wide_one[...] = in_one[...].astype(jnp.float32).reshape(count * padded, lanes)
-    mix(coef.astype(jnp.bfloat16), wide_one, wide_two, 1, seg_count, padded, both)
-    out_two[...] = wide_two[...].reshape(count, both, lanes).astype(jnp.bfloat16)
-    begin(second, count)
+    for p in (0, 1):
+        if p:
+            finish(first[1], count)
+        widen(in_one, wide_one, slim[p])
+        mix(coef.astype(jnp.bfloat16), p, wide_one, wide_two, 1, seg_count)
+        narrow(wide_two, out_two, double[p])
+        begin(second[p], count)
     in_two[pl.ds(me, 1)] = out_two[pl.ds(me, 1)]
 
     finish(gather_copy, sides)
@@ -199,10 +241,12 @@
         return carry
 
     lax.fori_loop(0, width // pair_lanes, seg_grads, 0)
-    begin(third, count)
+    begin(third[0], count)
+    begin(third[1], count)
     in_three[pl.ds(me, 1)] = out_three[pl.ds(me, 1)]
 
-    finish(second, count)
+    finish(second[0], count)
+    finish(second[1], count)
     wide_two[...] = in_two[...].astype(jnp.float32).reshape(count * both, lanes)
 
     def forward(block, carry):
@@ -249,14 +293,15 @@
 
     lax.fori_loop(0, tall // height, backward, 0)
 
-    finish(third, count)
     turned = jnp.transpose(coef)
     by_segment = jnp.concatenate([turned[:count], turned[count:]], axis=1)
-    wide_two[...] = in_three[...].astype(jnp.float32).reshape(count * both, lanes)
     wide_one[...] = jnp.zeros_like(wide_one)
-    mix(by_segment.astype(jnp.bfloat16), wide_two, wide_one, seg_count, 1, both, padded)
-    out_four[...] = wide_one[...].reshape(count, padded, lanes).astype(jnp.bfloat16)
-    begin(fourth, count)
+    for p in (0, 1):
+        finish(third[p], count)
+        widen(in_three, wide_two, double[p])
+        mix(by_segment.astype(jnp.bfloat16), p, wide_two, wide_one, seg_count, 1)
+        narrow(wide_one, out_four, slim[p])
+        begin(fourth[p], count)
     slot_ref[pl.ds(me, 1)] = out_four[pl.ds(me, 1)]
 
     finish(scatter_copy, sides)
@@ -270,7 +315,8 @@
         return carry
 
     lax.fori_loop(0, tall // height, add_up, 0)
-    finish(fourth, count)
+    finish(fourth[0], count)
+    finish(fourth[1], count)
 
 
 def whole_step(blocks, place, cotangent, hidden, hidden_t, rows, seg_count, decode):
@@ -304,7 +350,7 @@
             narrow((high, part * sides)),
             narrow((tall, part * sides)),
         ]
-        + [pltpu.SemaphoreType.DMA((count,))] * 8
+        + [pltpu.SemaphoreType.DMA((2 * count,))] * 8
         + [pltpu.SemaphoreType.DMA((sides,))] * 4,
         compiler_params=pltpu.CompilerParams(
             collective_id=0, has_side_effects=True, vmem_limit_bytes=56 * 1024 * 1024
@@ -330,7 +376,7 @@
     meta = jnp.pad(meta[None, :], ((0, padded - rows - 1), (0, lanes - 3 * listed)))
     table_chunks = split_panels(jnp.transpose(down_table, (1, 0, 2)), count)
     outgoing = jnp.concatenate(
-        [table_chunks, jnp.broadcast_to(meta, (count,) + meta.shape)], axis=1
+        [jnp.broadcast_to(meta, (count,) + meta.shape), table_chunks], axis=1
     )
     slot_range = jnp.arange(count, dtype=jnp.int32)
     place = jnp.pad(
@@ -345,9 +391,14 @@
         ],
         axis=0,
     )
+    cut = padded // 2 - (padded - rows)
     parts = hidden_act.reshape(seg_count, seg_len, ROW_PARTS, 1, rows)
     same = jnp.eye(seg_count, dtype=jnp.bool_)[:, None, None, :, None]
-    hidden = jnp.where(same, parts, 0).reshape(row_count, ROW_PARTS * seg_count * rows)
+    spread = jnp.where(same, parts, 0)
+    lead_shape = (row_count, ROW_PARTS, -1)
+    hidden = jnp.concatenate(
+        [spread[..., :cut].reshape(lead_shape), spread[..., cut:].reshape(lead_shape)], axis=2
+    ).reshape(row_count, ROW_PARTS * seg_count * rows)
     slot_chunks, layer_out, grad_all = whole_step(
         outgoing,
         place_two,
@@ -356,11 +407,21 @@
         hidden.T,
         rows,
         seg_count,
-        (rows, listed, seg_count),
-    )
-    grad_view = grad_all.reshape(seg_count, seg_len, ROW_PARTS, seg_count, rows)
+        (0, listed, seg_count),
+    )
+    grad_view = grad_all.reshape(seg_count, seg_len, ROW_PARTS, seg_count * rows)
+    low, rest = seg_count * cut, rows - cut
     grad_hidden = jnp.stack(
-        [grad_view[seg, :, :, seg] for seg in range(seg_count)]
+        [
+            jnp.concatenate(
+                [
+                    grad_view[seg, :, :, seg * cut : (seg + 1) * cut],
+                    grad_view[seg, :, :, low + seg * rest : low + (seg + 1) * rest],
+                ],
+                axis=2,
+            )
+            for seg in range(seg_count)
+        ]
     ).reshape(row_count, ff_local)
     own_grad = join_panels(slot_chunks, 1, rows)
     expert_grad = jnp.transpose(own_grad, (1, 0, 2)).astype(jnp.float32)

time: 148 us -> 146 us (0.986)
  the two profiles are of different devices: /device:TPU:143 before, /device:TPU:1 now
where the time goes in v2:
time: 146 us; the launch traced here: 145 us
  Pallas kernels  131 us (90%)
  local copies, waits for them, and re-layouts  8.11 us (6%)
  other arithmetic  4.6 us (3%)
    pallas_call x1, Pallas kernels, whole_step(): pl.pallas_call(functools.partial(step_body, rows, seg_count, decode), out...  131 us

profile of v2, /device:TPU:1, one launch (start us, length us, event | category | flops | bytes accessed | tf_op | source)
XLA Modules:
  0.0 145.1 jit_solution(12760864545700047265)
XLA Ops:
  0.6 0.7 convert_convert_fusion
  1.4 0.7 reduce-precision_convert_fusion
  2.3 0.7 iota_compare_fusion.2
  3.1 0.7 fusion.2.place_ref
  3.8 1.0 broadcast_in_dim.32
  4.8 0.3 broadcast_select_fusion
  5.1 0.1 slice.28
  5.3 0.1 slice.29
  5.4 0.1 reshape.104
  5.5 0.1 reshape.103
  5.7 0.9 copy.34.hid_ref
  6.7 0.1 copy.44
  6.8 0.2 copy.33
  7.0 1.2 pad_maximum_fusion.x_ref
  8.2 131.5 %shard_map.85 = (bf16[64,48,128]{2,1,0:T(8,128)(2,1)}, bf16[512,256]{1,0:T(8,128)(2,1)}, bf16[512,352]{1,0:T(8,128)(2,1)}) custom-call(bf16[64,48,128]{2,1,0:T(8,128)(2,1)} %pad_maximum_fusion.x_ref, bf16[256,128]{1,0:T(8,128)(2,1)} %fusion.2.place_ref, bf16[512,256]{1,0:T(8,128)(2,1)} %cot_ref.1, bf16[512,352]{1,0:T(8,128)(2,1)} %copy.34.hid_ref, ...), custom_call_target="tpu_custom_call" | custom-call | tf_op jit(solution)/shard_map/pallas_call | solution.py:334
  139.7 1.2 copy.35
  140.9 0.1 fusion.14
  141.1 0.2 fusion.15
  141.5 0.2 copy.40
  141.7 0.7 copy.45
  142.4 0.3 slice.27
  142.7 0.1 convert_bitcast_fusion
  142.8 1.5 %copy.41 = f32[1,4,44,16,128]{4,3,2,1,0:T(8,128)} copy(f32[1,4,44,16,128]{4,2,3,1,0:T(8,128)S(1)} %convert_bitcast_fusion) | data formatting | bytes 2883584 | tf_op jit(solution)/shard_map/convert_element_type | solution.py:427
  144.4 0.7 copy.52
  (25 shorter events, 0.6 us)
Async XLA Ops:
  5.1 1.5 %copy-start.2 = (bf16[176,1,2048]{2,0,1:T(8,128)(2,1)S(1)}, bf16[176,1,2048]{2,0,1:T(8,128)(2,1)}, u32[]{:S(2)}) copy-start(bf16[176,1,2048]{2,0,1:T(8,128)(2,1)} %param.8) | copy-start | bytes 2162692
  5.7 1.3 copy-start
  140.9 1.4 copy-start.1
  142.8 1.6 %copy-start.3 = (bf16[512,256]{1,0:T(8,128)(2,1)S(1)}, bf16[512,256]{1,0:T(8,128)(2,1)}, u32[]{:S(2)}) copy-start(bf16[512,256]{1,0:T(8,128)(2,1)} %get-tuple-element.22) | copy-start | bytes 786436

commit v3 on v2

--- a/solution.py
+++ b/solution.py
@@ -99,7 +99,8 @@
 
     def copies(source, target, send_sem, recv_sem, piece, piece_index):
         def copy(step):
-            peer = lax.rem(me + step, count)
+            swing = lax.div(step, 2) * (1 - 2 * lax.rem(step, 2))
+            peer = lax.rem(me + count // 2 + swing, count)
             mark = piece_index * count + step
             return pltpu.make_async_remote_copy(
                 src_ref=source.at[peer, pl.ds(*piece)],

time: 146 us -> 147 us (level)
  Pallas kernels: 131 us -> 133 us
where the time goes in v3:
time: 147 us; the launch traced here: 146 us
  Pallas kernels  133 us (90%)
  local copies, waits for them, and re-layouts  8.11 us (6%)
  other arithmetic  4.6 us (3%)
    pallas_call x1, Pallas kernels, whole_step(): pl.pallas_call(functools.partial(step_body, rows, seg_count, decode), out...  133 us

profile of v3, /device:TPU:1, one launch (start us, length us, event | category | flops | bytes accessed | tf_op | source)
XLA Modules:
  0.0 146.5 jit_solution(1728577753822054667)
XLA Ops:
  0.6 0.7 convert_convert_fusion
  1.4 0.7 reduce-precision_convert_fusion
  2.3 0.7 iota_compare_fusion.2
  3.1 0.7 fusion.2.place_ref
  3.8 1.0 broadcast_in_dim.32
  4.8 0.3 broadcast_select_fusion
  5.1 0.1 slice.28
  5.3 0.1 slice.29
  5.4 0.1 reshape.104
  5.5 0.1 reshape.103
  5.7 0.9 copy.34.hid_ref
  6.7 0.1 copy.44
  6.8 0.2 copy.33
  7.0 1.2 pad_maximum_fusion.x_ref
  8.2 132.9 %shard_map.85 = (bf16[64,48,128]{2,1,0:T(8,128)(2,1)}, bf16[512,256]{1,0:T(8,128)(2,1)}, bf16[512,352]{1,0:T(8,128)(2,1)}) custom-call(bf16[64,48,128]{2,1,0:T(8,128)(2,1)} %pad_maximum_fusion.x_ref, bf16[256,128]{1,0:T(8,128)(2,1)} %fusion.2.place_ref, bf16[512,256]{1,0:T(8,128)(2,1)} %cot_ref.1, bf16[512,352]{1,0:T(8,128)(2,1)} %copy.34.hid_ref, ...), custom_call_target="tpu_custom_call" | custom-call | tf_op jit(solution)/shard_map/pallas_call | solution.py:335
  141.1 1.2 copy.35
  142.3 0.1 fusion.14
  142.5 0.2 fusion.15
  142.9 0.2 copy.40
  143.1 0.7 copy.45
  143.8 0.3 slice.27
  144.1 0.1 convert_bitcast_fusion
  144.2 1.5 %copy.41 = f32[1,4,44,16,128]{4,3,2,1,0:T(8,128)} copy(f32[1,4,44,16,128]{4,2,3,1,0:T(8,128)S(1)} %convert_bitcast_fusion) | data formatting | bytes 2883584 | tf_op jit(solution)/shard_map/convert_element_type | solution.py:428
  145.8 0.7 copy.52
  (25 shorter events, 0.6 us)
Async XLA Ops:
  5.1 1.5 %copy-start.2 = (bf16[176,1,2048]{2,0,1:T(8,128)(2,1)S(1)}, bf16[176,1,2048]{2,0,1:T(8,128)(2,1)}, u32[]{:S(2)}) copy-start(bf16[176,1,2048]{2,0,1:T(8,128)(2,1)} %param.8) | copy-start | bytes 2162692
  5.7 1.3 copy-start
  142.3 1.4 copy-start.1
  144.2 1.6 %copy-start.3 = (bf16[512,256]{1,0:T(8,128)(2,1)S(1)}, bf16[512,256]{1,0:T(8,128)(2,1)}, u32[]{:S(2)}) copy-start(bf16[512,256]{1,0:T(8,128)(2,1)} %get-tuple-element.22) | copy-start | bytes 786436
